TPU v7x, 32 devices: a whole 2x2x4 slice. The times are simulated.
32 devices in a mesh: tm: 4 (over y, x), space: 8 (over z, core).
Axes of the slice: x: 2, y: 2, z: 4, core: 2. Of those that a mesh axis runs over, the one named last changes fastest.
Arguments:
- pixel_cot: bfloat16 [16, 64, 64, 128], P('tm', 'space'), may hold values from -6 to 6
- frame_group: int32 [16], P('tm'), may hold values from 0 to 3
- advantage: float32 [4], replicated, may hold values from -4 to 4
- block_in: bfloat16 [2, 16, 64, 64, 128], P(None, 'tm', 'space'), may hold values from -6 to 6
- conv1_weight: bfloat16 [2, 3, 3, 3, 128, 128], replicated, may hold values from -0.109375 to 0.109375
- conv2_weight: bfloat16 [2, 3, 3, 3, 128, 128], replicated, may hold values from -0.109375 to 0.109375
- owner_map: int32 [4, 8, 64, 1], P('tm', 'space'), may hold values from 0 to 7; in each aligned block of 64 rows (0 to 63, 64 to 127, ..., all dimensions but the last counted through in order) at most 16 rows name the same one
Outputs:
- latent_grad: bfloat16 [4, 8, 8, 16, 1024], P('tm', 'space')
Inputs may be any that keep to these rules, and one draw needn't show every extreme that they name: `owner_map`: among the units of one device, at most 16 have the same owner, and in some devices exactly 16 do.
All inputs are finite; a program needn't handle non-finite values.
Results may differ from a plain program's by a relative error of at most 0.013.
Values may be sent and summed in bfloat16 or wider, within the bound.
A program may use at most 128 MiB of HBM per device.

v0:
```python
import functools

import jax
import jax.numpy as jnp
from jax import lax
from jax.experimental import pallas as pl
from jax.experimental.pallas import tpu as pltpu
from jax.sharding import PartitionSpec as P

F32 = jnp.float32
BF16 = jnp.bfloat16


def kernel(
    cot, group, adv, block_in, w1_hbm, w2_hbm, owner, out,
    w1, w2, fields, x_past, x_up, x_gr, pre_acc, grad_acc, pool_a, pool_b, outgoing,
    send_sem, recv_sem, a2a_send, a2a_recv, local_sem,
):
    frames, rows, cols, chan = cot.shape
    blocks = block_in.shape[0]
    pairs = frames // 2
    pixels = rows * cols
    n_tm, n_sp = lax.axis_size("tm"), lax.axis_size("space")
    tm, sp = lax.axis_index("tm"), lax.axis_index("space")
    yes = tm >= 0

    def up_field(layer):
        return blocks + 2 * layer

    def gr_field(layer):
        return blocks + 2 * layer + 1

    low, high = sp > 0, sp < n_sp - 1
    before, after = tm > 0, tm < n_tm - 1

    def remote(src, dst, field, channel, dtm, dsp):
        return pltpu.make_async_remote_copy(
            src_ref=src, dst_ref=dst,
            send_sem=send_sem.at[field, channel], recv_sem=recv_sem.at[field, channel],
            device_id={"tm": tm + dtm, "space": sp + dsp},
            device_id_type=pl.DeviceIdType.MESH,
        )

    def time_copies(field, past):
        buf = fields.at[field]
        if past:
            src = lambda r, n: block_in.at[field, frames - 2 : frames, r : r + n]
            dst = lambda r, n: buf.at[0:2, r : r + n]
            d, can, get = 1, after, before
        else:
            src = lambda r, n: buf.at[0:2, r + 1 : r + 1 + n]
            dst = lambda r, n: buf.at[frames : frames + 2, r : r + n]
            d, can, get = -1, before, after
        return [
            (remote(src(0, rows), dst(1, rows), field, 0, d, 0), can, get),
            (remote(src(0, 1), dst(rows + 1, 1), field, 1, d, -1), can & low, get & high),
            (remote(src(rows - 1, 1), dst(0, 1), field, 2, d, 1), can & high, get & low),
        ]

    def row_copies(field, past, pair):
        buf = fields.at[field]
        if past:
            src = lambda r: block_in.at[field, 2 * pair : 2 * pair + 2, r : r + 1]
            dst = lambda r: buf.at[2 + 2 * pair : 4 + 2 * pair, r : r + 1]
        else:
            src = lambda r: buf.at[2 * pair : 2 * pair + 2, r + 1 : r + 2]
            dst = lambda r: buf.at[2 * pair : 2 * pair + 2, r : r + 1]
        return [
            (remote(src(0), dst(rows + 1), field, 3 + 2 * pair, 0, -1), low, high),
            (remote(src(rows - 1), dst(0), field, 4 + 2 * pair, 0, 1), high, low),
        ]

    def start(copies):
        for copy, sends, _ in copies:
            pl.when(sends)(copy.start)

    def arrive(copies):
        for copy, _, gets in copies:
            pl.when(gets)(copy.wait_recv)

    def sent(copies):
        for copy, sends, _ in copies:
            pl.when(sends)(copy.wait_send)

    loads = {}

    def load(name, src, dst, number):
        loads[name] = pltpu.make_async_copy(src, dst, local_sem.at[number])
        loads[name].start()

    last = blocks - 1
    load("cot", cot, fields.at[up_field(last), 0:frames, 1 : rows + 1], 0)
    for layer in reversed(range(blocks)):
        load(("in", layer), block_in.at[layer], fields.at[layer, 2 : frames + 2, 1 : rows + 1], 1 + layer)
        load(("w1", layer), w1_hbm.at[layer], w1.at[layer], 1 + blocks + layer)
        load(("w2", layer), w2_hbm.at[layer], w2.at[layer], 1 + 2 * blocks + layer)

    pair_range = range(pairs)
    start(row_copies(last, True, pairs - 1))
    for pair in reversed(range(pairs - 1)):
        start(row_copies(last, True, pair))
    start(time_copies(last, True))

    at_col = lax.broadcasted_iota(jnp.int32, (cols, chan), 0)

    def spread(x, frame, row, value):
        wide = value.astype(F32)
        left = jnp.where(at_col == 0, 0.0, pltpu.roll(wide, 1, axis=0))
        right = jnp.where(at_col == cols - 1, 0.0, pltpu.roll(wide, cols - 1, axis=0))
        x[frame, row, :, 0:chan] = left.astype(BF16)
        x[frame, row, :, chan : 2 * chan] = value
        x[frame, row, :, 2 * chan : 3 * chan] = right.astype(BF16)

    def clear(x, frame, row):
        x[frame, row] = jnp.zeros((cols, 3 * chan), BF16)

    def edge(x, field, frame, row, present):
        @pl.when(present)
        def _():
            spread(x, frame, row, fields[field, frame, row])

        @pl.when(jnp.logical_not(present))
        def _():
            clear(x, frame, row)

    def row_edges(x, field, past, pair):
        arrive(row_copies(field, past, pair))
        for i in range(2):
            frame = 2 * pair + i + (2 if past else 0)
            edge(x, field, frame, 0, low)
            edge(x, field, frame, rows + 1, high)

    def time_edges(x, field, past):
        arrive(time_copies(field, past))
        present = before if past else after
        for i in range(2):
            frame = i if past else frames + i

            @pl.when(present)
            def _():
                @pl.loop(1, rows + 1)
                def _(row):
                    spread(x, frame, row, fields[field, frame, row])

            @pl.when(jnp.logical_not(present))
            def _():
                @pl.loop(1, rows + 1)
                def _(row):
                    clear(x, frame, row)

            edge(x, field, frame, 0, present & low)
            edge(x, field, frame, rows + 1, present & high)

    def own_rows(x, field, past):
        @pl.loop(0, frames * rows)
        def _(at):
            frame = at // rows + (2 if past else 0)
            row = at % rows + 1
            spread(x, frame, row, fields[field, frame, row])

    def tap(w, layer, a, flip):
        if not flip:
            return w[layer, a].reshape(9 * chan, chan)
        return jnp.concatenate([w[layer, a, 2 - r, 2 - s] for r in range(3) for s in range(3)], axis=1)

    def conv(acc, x, w, layer, flip, pair, order, hooks):
        zero = jnp.zeros((chan, 9 * chan) if flip else (9 * chan, chan), BF16)
        outer = 0 if flip else 1
        for step, group_of in enumerate(order):
            lhs, rhs = [], []
            for j in group_of:
                if j in hooks:
                    hooks[j]()
            for j in group_of:
                lhs += [x[2 * pair + j, r : r + rows].reshape(pixels, 3 * chan) for r in range(3)]
                taps = [(2 - k if flip else k) if 0 <= k <= 2 else None for k in (j, j - 1)]
                parts = [zero if a is None else tap(w, layer, a, flip) for a in taps]
                rhs.append(jnp.concatenate(parts, axis=outer))
            left = jnp.concatenate(lhs, axis=1)
            right = jnp.concatenate(rhs, axis=1 if flip else 0)
            dims = (((1,), (1,)), ((), ())) if flip else (((1,), (0,)), ((), ()))
            value = lax.dot_general(left, right, dims, preferred_element_type=F32)
            if step == 0:
                acc[...] = value
            else:
                acc[...] += value

    def conv_past(layer, pair):
        order, hooks = ((0, 1), (2, 3)), {}
        if pair == 0:
            order, hooks = ((2, 3), (0, 1)), {0: lambda: time_edges(x_past, layer, True)}
        conv(pre_acc.at[layer, pair], x_past, w1, layer, False, pair, order, hooks)

    def conv_future(x, w, layer, field, pair):
        hooks = {}
        if pair == 0:
            hooks[0] = lambda: row_edges(x, field, False, 0)
        if pair < pairs - 1:
            hooks[2] = lambda: row_edges(x, field, False, pair + 1)
        else:
            hooks[2] = lambda: time_edges(x, field, False)
        conv(grad_acc.at[pair], x, w, layer, True, pair, ((0, 1), (2, 3)), hooks)

    def send(field, pair):
        if pair == 0:
            start(time_copies(field, False))
        start(row_copies(field, False, pair))

    loads["cot"].wait()
    for frame in range(frames):
        scale = adv[group[frame]]

        @pl.loop(1, rows + 1)
        def _(row):
            value = (fields[up_field(last), frame, row].astype(F32) * scale).astype(BF16)
            fields[up_field(last), frame, row] = value
            spread(x_up, frame, row, value)

        if frame % 2 == 1:
            send(up_field(last), frame // 2)

    def grad_pre(layer, pair):
        field = gr_field(layer)
        for i in range(2):
            @pl.loop(0, rows)
            def _(row):
                at = pl.ds(pl.multiple_of(row * cols, cols), cols)
                lanes = slice(i * chan, (i + 1) * chan)
                grad = grad_acc[pair, at, lanes]
                pre = pre_acc[layer, pair, at, lanes]
                s = jax.nn.sigmoid(pre)
                value = (grad * (s * (1.0 + pre * (1.0 - s)))).astype(BF16)
                fields[field, 2 * pair + i, row + 1] = value
                spread(x_gr, 2 * pair + i, row + 1, value)
        send(field, pair)

    def next_up(layer, pair):
        field = up_field(layer - 1)
        for i in range(2):
            @pl.loop(0, rows)
            def _(row):
                at = pl.ds(pl.multiple_of(row * cols, cols), cols)
                back = grad_acc[pair, at, i * chan : (i + 1) * chan]
                value = (fields[up_field(layer), 2 * pair + i, row + 1].astype(F32) + back).astype(BF16)
                fields[field, 2 * pair + i, row + 1] = value
                spread(x_up, 2 * pair + i, row + 1, value)
        send(field, pair)

    def pool(layer, pair):
        for i in range(2):
            @pl.loop(0, rows // 2)
            def _(r):
                total = jnp.zeros((cols, chan), F32)
                for k in range(2):
                    row = 2 * r + k
                    at = pl.ds(pl.multiple_of(row * cols, cols), cols)
                    back = grad_acc[pair, at, i * chan : (i + 1) * chan]
                    value = fields[up_field(layer), 2 * pair + i, row + 1].astype(F32) + back
                    total = total + value.astype(BF16).astype(F32)
                at = pl.multiple_of(((2 * pair + i) * (rows // 2) + r) * cols, cols)
                pool_a[pl.ds(at, cols), :] = total

    def load_block(layer):
        loads[("in", layer)].wait()
        own_rows(x_past, layer, True)
        for pair in reversed(pair_range):
            row_edges(x_past, layer, True, pair)

    for layer in reversed(range(blocks)):
        up, gr = up_field(layer), gr_field(layer)
        if layer == last:
            load_block(layer)
            loads[("w1", layer)].wait()
            for pair in reversed(range(1, pairs)):
                conv_past(layer, pair)
        loads[("w2", layer)].wait()
        conv_future(x_up, w2, layer, up, 0)
        if layer == last:
            conv_past(layer, 0)
            for nxt in reversed(range(last)):
                for pair in reversed(pair_range):
                    start(row_copies(nxt, True, pair))
                start(time_copies(nxt, True))
        grad_pre(layer, 0)
        for pair in range(1, pairs):
            conv_future(x_up, w2, layer, up, pair)
            grad_pre(layer, pair)
        if layer > 0:
            load_block(layer - 1)
            loads[("w1", layer - 1)].wait()
            for pair in reversed(pair_range):
                conv_past(layer - 1, pair)
        for pair in pair_range:
            conv_future(x_gr, w1, layer, gr, pair)
            if layer > 0:
                next_up(layer, pair)
            else:
                pool(layer, pair)

    units_n = owner.shape[1]
    cap = out.shape[3]
    places = n_sp * cap
    lat = pool_b.shape[0]
    even = pool_a[pl.ds(0, lat, stride=2), :]
    odd = pool_a[pl.ds(1, lat, stride=2), :]
    pool_b[...] = (even + odd).astype(BF16).astype(F32)
    wide = lat // units_n
    units = jnp.concatenate(
        [pool_b[pl.ds(k, units_n, stride=wide), :] for k in range(wide)], axis=1
    ).astype(BF16)
    owners = owner[...]
    hot = jnp.where(owners == lax.broadcasted_iota(jnp.int32, (128, units_n), 0), 1.0, 0.0)
    tri = jnp.where(
        lax.broadcasted_iota(jnp.int32, (units_n, units_n), 0)
        <= lax.broadcasted_iota(jnp.int32, (units_n, units_n), 1), 1.0, 0.0,
    )
    ranks = jnp.dot(hot.astype(BF16), tri.astype(BF16), preferred_element_type=F32)
    position = jnp.sum(ranks * hot, axis=0, keepdims=True) - 1.0
    slot = owners.astype(F32) * cap + position
    chosen = jnp.where(
        slot == lax.broadcasted_iota(jnp.int32, (places, units_n), 0).astype(F32), 1.0, 0.0
    )
    placed = jnp.dot(chosen.astype(BF16), units, preferred_element_type=F32)
    for o in range(n_sp):
        outgoing[o] = placed[o * cap : (o + 1) * cap].astype(BF16)

    mine = pltpu.make_async_copy(outgoing.at[sp], out.at[0, 0, sp], local_sem.at[1 + 3 * blocks])
    mine.start()
    moves = []
    for k in range(1, n_sp):
        to = lax.rem(sp + k, n_sp)
        copy = pltpu.make_async_remote_copy(
            src_ref=outgoing.at[to], dst_ref=out.at[0, 0, sp],
            send_sem=a2a_send.at[k], recv_sem=a2a_recv.at[k],
            device_id={"space": to}, device_id_type=pl.DeviceIdType.MESH,
        )
        copy.start()
        moves.append(copy)
    mine.wait()
    for k, copy in enumerate(moves, 1):
        copy.wait_send()
        came = lax.rem(sp - k + n_sp, n_sp)
        pltpu.make_async_remote_copy(
            src_ref=outgoing.at[came], dst_ref=out.at[0, 0, came],
            send_sem=a2a_send.at[k], recv_sem=a2a_recv.at[k],
            device_id={"space": came}, device_id_type=pl.DeviceIdType.MESH,
        ).wait_recv()
    for layer in range(blocks):
        sent(time_copies(layer, True))
        for field in (up_field(layer), gr_field(layer)):
            sent(time_copies(field, False))
        for pair in pair_range:
            sent(row_copies(layer, True, pair))
            for field in (up_field(layer), gr_field(layer)):
                sent(row_copies(field, False, pair))


def on_device(pixel_cot, frame_group, advantage, block_in, conv1_weight, conv2_weight, owner_map):
    frames, rows, cols, chan = pixel_cot.shape
    blocks = block_in.shape[0]
    pairs = frames // 2
    units = owner_map.shape[2]
    n_sp = lax.axis_size("space")
    cap = max(2, 2 * units // n_sp)
    unit = frames * (rows // 2) * (cols // 2) * chan // units
    lat = frames * (rows // 2) * (cols // 2)
    spread = (frames + 2, rows + 2, cols, 3 * chan)
    smem = pl.BlockSpec(memory_space=pltpu.SMEM)
    hbm = pl.BlockSpec(memory_space=pl.ANY)
    vmem = pl.BlockSpec(memory_space=pltpu.VMEM)
    return pl.pallas_call(
        kernel,
        out_shape=jax.ShapeDtypeStruct((1, 1, n_sp, cap, unit), BF16),
        in_specs=[hbm, smem, smem, hbm, hbm, hbm, vmem],
        out_specs=hbm,
        scratch_shapes=[
            pltpu.VMEM(conv1_weight.shape, BF16),
            pltpu.VMEM(conv2_weight.shape, BF16),
            pltpu.VMEM((3 * blocks, frames + 2, rows + 2, cols, chan), BF16),
            pltpu.VMEM(spread, BF16),
            pltpu.VMEM(spread, BF16),
            pltpu.VMEM(spread, BF16),
            pltpu.VMEM((blocks, pairs, rows * cols, 2 * chan), F32),
            pltpu.VMEM((pairs, rows * cols, 2 * chan), F32),
            pltpu.VMEM((2 * lat, chan), F32),
            pltpu.VMEM((lat, chan), F32),
            pltpu.VMEM((n_sp, cap, unit), BF16),
            pltpu.SemaphoreType.DMA((3 * blocks, 3 + 2 * pairs)),
            pltpu.SemaphoreType.DMA((3 * blocks, 3 + 2 * pairs)),
            pltpu.SemaphoreType.DMA((n_sp,)),
            pltpu.SemaphoreType.DMA((n_sp,)),
            pltpu.SemaphoreType.DMA((2 + 3 * blocks,)),
        ],
        compiler_params=pltpu.CompilerParams(
            has_side_effects=True, vmem_limit_bytes=60 * 1024 * 1024
        ),
    )(pixel_cot, frame_group, advantage, block_in, conv1_weight, conv2_weight, owner_map.reshape(1, units))


def solution(mesh):
    in_specs = (
        P("tm", "space", None, None),
        P("tm"),
        P(),
        P(None, "tm", "space", None, None),
        P(),
        P(),
        P("tm", "space", None, None),
    )
    out_specs = P("tm", "space", None, None, None)
    return jax.shard_map(
        on_device, mesh=mesh, in_specs=in_specs, out_specs=out_specs, check_vma=False
    )
```

profile of v0, /device:TPU:1, one launch (start us, length us, event | category | flops | bytes accessed | tf_op | source)
XLA Modules:
  0.0 64.8 jit_solution(8690453703913342518)
XLA Ops:
  0.0 63.1 %shard_map.73 = bf16[1,1,8,16,1024]{4,3,2,1,0:T(8,128)(2,1)} custom-call(bf16[4,8,64,128]{3,2,1,0:T(8,128)(2,1)} %cot.1, s32[4]{0:T(128)} %group.1, f32[4]{0:T(128)} %adv.1, bf16[2,4,8,64,128]{4,3,2,1,0:T(8,128)(2,1)} %block_in.1, bf16[2,3,3,3,128,128]{5,4,3,2,1,0:T(8,128)(2,1)} %w1_hbm.1, bf16[2,3,3,3,128,128]{5,4,3,2,1,0:T(8,128)(2,1)} %w2_hbm.1, ...), custom_call_target="tpu_custom_call" | custom-call | tf_op jit(solution)/shard_map/pallas_call | solution.py:371
  63.1 1.7 %copy.9 = bf16[1,1,8,16,1024]{4,3,2,1,0:T(8,128)(2,1)} copy(bf16[1,1,8,16,1024]{4,3,2,1,0:T(8,128)(2,1)} %shard_map.73) | data formatting | bytes 524288
where the time goes:
time: 64.9 us; the launch traced here: 64.8 us
  Pallas kernels  63.1 us (97%)
  local copies, waits for them, and re-layouts  1.67 us (3%)
    pallas_call x1, Pallas kernels, on_device(): pl.pallas_call(kernel, out_shape=jax.ShapeDtypeStruct((1, 1, n_sp, cap, u...  63.1 us
    unnamed x1, local copies, waits for them, and re-layouts  1.67 us

commit v1 on v0

--- a/solution.py
+++ b/solution.py
@@ -95,6 +95,23 @@
         load(("w1", layer), w1_hbm.at[layer], w1.at[layer], 1 + blocks + layer)
         load(("w2", layer), w2_hbm.at[layer], w2.at[layer], 1 + 2 * blocks + layer)
 
+    barrier = pltpu.get_barrier_semaphore()
+
+    def greet(dtm, to):
+        pl.semaphore_signal(
+            barrier, inc=1, device_id={"tm": tm + dtm, "space": to},
+            device_id_type=pl.DeviceIdType.MESH,
+        )
+
+    for k in range(1, n_sp):
+        greet(0, lax.rem(sp + k, n_sp))
+    expected = n_sp - 1
+    for dtm, can in ((1, after), (-1, before)):
+        for dsp, there in ((0, yes), (-1, low), (1, high)):
+            pl.when(can & there)(functools.partial(greet, dtm, sp + dsp))
+            expected = expected + jnp.where(can & there, 1, 0)
+    pl.semaphore_wait(barrier, expected)
+
     pair_range = range(pairs)
     start(row_copies(last, True, pairs - 1))
     for pair in reversed(range(pairs - 1)):
@@ -166,24 +183,30 @@
     def conv(acc, x, w, layer, flip, pair, order, hooks):
         zero = jnp.zeros((chan, 9 * chan) if flip else (9 * chan, chan), BF16)
         outer = 0 if flip else 1
+
+        def part(j, r, half):
+            first = r + half * rows // 2
+            return x[2 * pair + j, first : first + rows // 2].reshape(pixels // 2, 3 * chan)
+
         for step, group_of in enumerate(order):
-            lhs, rhs = [], []
+            rhs = []
             for j in group_of:
                 if j in hooks:
                     hooks[j]()
             for j in group_of:
-                lhs += [x[2 * pair + j, r : r + rows].reshape(pixels, 3 * chan) for r in range(3)]
                 taps = [(2 - k if flip else k) if 0 <= k <= 2 else None for k in (j, j - 1)]
                 parts = [zero if a is None else tap(w, layer, a, flip) for a in taps]
                 rhs.append(jnp.concatenate(parts, axis=outer))
-            left = jnp.concatenate(lhs, axis=1)
             right = jnp.concatenate(rhs, axis=1 if flip else 0)
             dims = (((1,), (1,)), ((), ())) if flip else (((1,), (0,)), ((), ()))
-            value = lax.dot_general(left, right, dims, preferred_element_type=F32)
-            if step == 0:
-                acc[...] = value
-            else:
-                acc[...] += value
+            for half in range(2):
+                at = slice(half * pixels // 2, (half + 1) * pixels // 2)
+                left = jnp.concatenate([part(j, r, half) for j in group_of for r in range(3)], axis=1)
+                value = lax.dot_general(left, right, dims, preferred_element_type=F32)
+                if step == 0:
+                    acc[at] = value
+                else:
+                    acc[at] += value
 
     def conv_past(layer, pair):
         order, hooks = ((0, 1), (2, 3)), {}
@@ -392,7 +415,7 @@
             pltpu.SemaphoreType.DMA((2 + 3 * blocks,)),
         ],
         compiler_params=pltpu.CompilerParams(
-            has_side_effects=True, vmem_limit_bytes=60 * 1024 * 1024
+            has_side_effects=True, collective_id=0, vmem_limit_bytes=60 * 1024 * 1024
         ),
     )(pixel_cot, frame_group, advantage, block_in, conv1_weight, conv2_weight, owner_map.reshape(1, units))
 

time: 64.9 us -> 59.5 us (0.917)
  Pallas kernels: 63.1 us -> 57.4 us
    pallas_call x1, Pallas kernels: 63.1 us -> 57.4 us  [on_device(): pl.pallas_call(kernel, out_shape=jax.ShapeDtypeStruct((1, 1, n_sp, cap, u...]
where the time goes in v1:
time: 59.5 us; the launch traced here: 59.1 us
  Pallas kernels  57.4 us (96%)
  local copies, waits for them, and re-layouts  1.67 us (3%)
    pallas_call x1, Pallas kernels, on_device(): pl.pallas_call(kernel, out_shape=jax.ShapeDtypeStruct((1, 1, n_sp, cap, u...  57.4 us
    unnamed x1, local copies, waits for them, and re-layouts  1.67 us

profile of v1, /device:TPU:1, one launch (start us, length us, event | category | flops | bytes accessed | tf_op | source)
XLA Modules:
  0.0 59.1 jit_solution(9348277355915575042)
XLA Ops:
  0.0 57.4 %shard_map.73 = bf16[1,1,8,16,1024]{4,3,2,1,0:T(8,128)(2,1)} custom-call(bf16[4,8,64,128]{3,2,1,0:T(8,128)(2,1)} %cot.1, s32[4]{0:T(128)} %group.1, f32[4]{0:T(128)} %adv.1, bf16[2,4,8,64,128]{4,3,2,1,0:T(8,128)(2,1)} %block_in.1, bf16[2,3,3,3,128,128]{5,4,3,2,1,0:T(8,128)(2,1)} %w1_hbm.1, bf16[2,3,3,3,128,128]{5,4,3,2,1,0:T(8,128)(2,1)} %w2_hbm.1, ...), custom_call_target="tpu_custom_call" | custom-call | tf_op jit(solution)/shard_map/pallas_call | solution.py:394
  57.4 1.7 %copy.9 = bf16[1,1,8,16,1024]{4,3,2,1,0:T(8,128)(2,1)} copy(bf16[1,1,8,16,1024]{4,3,2,1,0:T(8,128)(2,1)} %shard_map.73) | data formatting | bytes 524288

commit v2 on v1

--- a/solution.py
+++ b/solution.py
@@ -22,7 +22,6 @@
     pixels = rows * cols
     n_tm, n_sp = lax.axis_size("tm"), lax.axis_size("space")
     tm, sp = lax.axis_index("tm"), lax.axis_index("space")
-    yes = tm >= 0
 
     def up_field(layer):
         return blocks + 2 * layer
@@ -51,10 +50,15 @@
             src = lambda r, n: buf.at[0:2, r + 1 : r + 1 + n]
             dst = lambda r, n: buf.at[frames : frames + 2, r : r + n]
             d, can, get = -1, before, after
+        return [(remote(src(0, rows), dst(1, rows), field, 0, d, 0), can, get)]
+
+    def corner_copies(field, past):
+        halo = fields.at[field, 0:2] if past else fields.at[field, frames : frames + 2]
+        here = before if past else after
+        row = lambda r: halo.at[:, r : r + 1]
         return [
-            (remote(src(0, rows), dst(1, rows), field, 0, d, 0), can, get),
-            (remote(src(0, 1), dst(rows + 1, 1), field, 1, d, -1), can & low, get & high),
-            (remote(src(rows - 1, 1), dst(0, 1), field, 2, d, 1), can & high, get & low),
+            (remote(row(1), row(rows + 1), field, 1, 0, -1), here & low, here & high),
+            (remote(row(rows), row(0), field, 2, 0, 1), here & high, here & low),
         ]
 
     def row_copies(field, past, pair):
@@ -107,16 +111,10 @@
         greet(0, lax.rem(sp + k, n_sp))
     expected = n_sp - 1
     for dtm, can in ((1, after), (-1, before)):
-        for dsp, there in ((0, yes), (-1, low), (1, high)):
-            pl.when(can & there)(functools.partial(greet, dtm, sp + dsp))
-            expected = expected + jnp.where(can & there, 1, 0)
-    pl.semaphore_wait(barrier, expected)
+        pl.when(can)(functools.partial(greet, dtm, sp))
+        expected = expected + jnp.where(can, 1, 0)
 
     pair_range = range(pairs)
-    start(row_copies(last, True, pairs - 1))
-    for pair in reversed(range(pairs - 1)):
-        start(row_copies(last, True, pair))
-    start(time_copies(last, True))
 
     at_col = lax.broadcasted_iota(jnp.int32, (cols, chan), 0)
 
@@ -147,8 +145,11 @@
             edge(x, field, frame, 0, low)
             edge(x, field, frame, rows + 1, high)
 
+    def accept(field, past):
+        arrive(time_copies(field, past))
+        start(corner_copies(field, past))
+
     def time_edges(x, field, past):
-        arrive(time_copies(field, past))
         present = before if past else after
         for i in range(2):
             frame = i if past else frames + i
@@ -165,6 +166,9 @@
                 def _(row):
                     clear(x, frame, row)
 
+        arrive(corner_copies(field, past))
+        for i in range(2):
+            frame = i if past else frames + i
             edge(x, field, frame, 0, present & low)
             edge(x, field, frame, rows + 1, present & high)
 
@@ -224,50 +228,64 @@
             hooks[2] = lambda: time_edges(x, field, False)
         conv(grad_acc.at[pair], x, w, layer, True, pair, ((0, 1), (2, 3)), hooks)
 
-    def send(field, pair):
+    def make(field, pair, each):
+        for i in range(2):
+            for row in (0, rows - 1):
+                each(i, row)
+        start(row_copies(field, False, pair))
+        for i in range(2):
+            pl.loop(1, rows - 1, unroll=2)(functools.partial(each, i))
         if pair == 0:
             start(time_copies(field, False))
-        start(row_copies(field, False, pair))
+
+    def place(row):
+        return pl.ds(pl.multiple_of(row * cols, cols), cols)
+
+    pl.semaphore_wait(barrier, expected)
+    start(time_copies(last, True))
+    for layer in reversed(range(blocks)):
+        for pair in reversed(pair_range):
+            start(row_copies(layer, True, pair))
+
+    def scaled(pair):
+        def each(i, row):
+            frame = 2 * pair + i
+            scale = adv[group[frame]]
+            value = (fields[up_field(last), frame, row + 1].astype(F32) * scale).astype(BF16)
+            fields[up_field(last), frame, row + 1] = value
+            spread(x_up, frame, row + 1, value)
+
+        make(up_field(last), pair, each)
 
     loads["cot"].wait()
-    for frame in range(frames):
-        scale = adv[group[frame]]
-
-        @pl.loop(1, rows + 1)
-        def _(row):
-            value = (fields[up_field(last), frame, row].astype(F32) * scale).astype(BF16)
-            fields[up_field(last), frame, row] = value
-            spread(x_up, frame, row, value)
-
-        if frame % 2 == 1:
-            send(up_field(last), frame // 2)
+    for pair in pair_range:
+        scaled(pair)
 
     def grad_pre(layer, pair):
         field = gr_field(layer)
-        for i in range(2):
-            @pl.loop(0, rows)
-            def _(row):
-                at = pl.ds(pl.multiple_of(row * cols, cols), cols)
-                lanes = slice(i * chan, (i + 1) * chan)
-                grad = grad_acc[pair, at, lanes]
-                pre = pre_acc[layer, pair, at, lanes]
-                s = jax.nn.sigmoid(pre)
-                value = (grad * (s * (1.0 + pre * (1.0 - s)))).astype(BF16)
-                fields[field, 2 * pair + i, row + 1] = value
-                spread(x_gr, 2 * pair + i, row + 1, value)
-        send(field, pair)
+
+        def each(i, row):
+            at = place(row)
+            lanes = slice(i * chan, (i + 1) * chan)
+            grad = grad_acc[pair, at, lanes]
+            pre = pre_acc[layer, pair, at, lanes]
+            s = jax.nn.sigmoid(pre)
+            value = (grad * (s * (1.0 + pre * (1.0 - s)))).astype(BF16)
+            fields[field, 2 * pair + i, row + 1] = value
+            spread(x_gr, 2 * pair + i, row + 1, value)
+
+        make(field, pair, each)
 
     def next_up(layer, pair):
         field = up_field(layer - 1)
-        for i in range(2):
-            @pl.loop(0, rows)
-            def _(row):
-                at = pl.ds(pl.multiple_of(row * cols, cols), cols)
-                back = grad_acc[pair, at, i * chan : (i + 1) * chan]
-                value = (fields[up_field(layer), 2 * pair + i, row + 1].astype(F32) + back).astype(BF16)
-                fields[field, 2 * pair + i, row + 1] = value
-                spread(x_up, 2 * pair + i, row + 1, value)
-        send(field, pair)
+
+        def each(i, row):
+            back = grad_acc[pair, place(row), i * chan : (i + 1) * chan]
+            value = (fields[up_field(layer), 2 * pair + i, row + 1].astype(F32) + back).astype(BF16)
+            fields[field, 2 * pair + i, row + 1] = value
+            spread(x_up, 2 * pair + i, row + 1, value)
+
+        make(field, pair, each)
 
     def pool(layer, pair):
         for i in range(2):
@@ -283,37 +301,37 @@
                 at = pl.multiple_of(((2 * pair + i) * (rows // 2) + r) * cols, cols)
                 pool_a[pl.ds(at, cols), :] = total
 
-    def load_block(layer):
+    def past_ahead(layer):
         loads[("in", layer)].wait()
         own_rows(x_past, layer, True)
         for pair in reversed(pair_range):
             row_edges(x_past, layer, True, pair)
-
+        loads[("w1", layer)].wait()
+        for pair in reversed(range(1, pairs)):
+            conv_past(layer, pair)
+
+    past_ahead(last)
     for layer in reversed(range(blocks)):
         up, gr = up_field(layer), gr_field(layer)
-        if layer == last:
-            load_block(layer)
-            loads[("w1", layer)].wait()
-            for pair in reversed(range(1, pairs)):
-                conv_past(layer, pair)
         loads[("w2", layer)].wait()
+        if layer < last:
+            accept(layer, True)
         conv_future(x_up, w2, layer, up, 0)
         if layer == last:
-            conv_past(layer, 0)
-            for nxt in reversed(range(last)):
-                for pair in reversed(pair_range):
-                    start(row_copies(nxt, True, pair))
-                start(time_copies(nxt, True))
+            accept(layer, True)
+        conv_past(layer, 0)
         grad_pre(layer, 0)
+        if layer > 0:
+            start(time_copies(layer - 1, True))
+            past_ahead(layer - 1)
         for pair in range(1, pairs):
+            if pair == pairs - 1:
+                accept(up, False)
             conv_future(x_up, w2, layer, up, pair)
             grad_pre(layer, pair)
-        if layer > 0:
-            load_block(layer - 1)
-            loads[("w1", layer - 1)].wait()
-            for pair in reversed(pair_range):
-                conv_past(layer - 1, pair)
         for pair in pair_range:
+            if pair == pairs - 1:
+                accept(gr, False)
             conv_future(x_gr, w1, layer, gr, pair)
             if layer > 0:
                 next_up(layer, pair)
@@ -370,8 +388,10 @@
         ).wait_recv()
     for layer in range(blocks):
         sent(time_copies(layer, True))
+        sent(corner_copies(layer, True))
         for field in (up_field(layer), gr_field(layer)):
             sent(time_copies(field, False))
+            sent(corner_copies(field, False))
         for pair in pair_range:
             sent(row_copies(layer, True, pair))
             for field in (up_field(layer), gr_field(layer)):

time: 59.5 us -> 55.1 us (0.926)
  Pallas kernels: 57.4 us -> 53.3 us
    pallas_call x1, Pallas kernels: 57.4 us -> 53.3 us  [on_device(): pl.pallas_call(kernel, out_shape=jax.ShapeDtypeStruct((1, 1, n_sp, cap, u...]
where the time goes in v2:
time: 55.1 us; the launch traced here: 55 us
  Pallas kernels  53.3 us (97%)
  local copies, waits for them, and re-layouts  1.67 us (3%)
    pallas_call x1, Pallas kernels, on_device(): pl.pallas_call(kernel, out_shape=jax.ShapeDtypeStruct((1, 1, n_sp, cap, u...  53.3 us
    unnamed x1, local copies, waits for them, and re-layouts  1.67 us

profile of v2, /device:TPU:1, one launch (start us, length us, event | category | flops | bytes accessed | tf_op | source)
XLA Modules:
  0.0 55.0 jit_solution(1464872734686048752)
XLA Ops:
  0.0 53.3 %shard_map.73 = bf16[1,1,8,16,1024]{4,3,2,1,0:T(8,128)(2,1)} custom-call(bf16[4,8,64,128]{3,2,1,0:T(8,128)(2,1)} %cot.1, s32[4]{0:T(128)} %group.1, f32[4]{0:T(128)} %adv.1, bf16[2,4,8,64,128]{4,3,2,1,0:T(8,128)(2,1)} %block_in.1, bf16[2,3,3,3,128,128]{5,4,3,2,1,0:T(8,128)(2,1)} %w1_hbm.1, bf16[2,3,3,3,128,128]{5,4,3,2,1,0:T(8,128)(2,1)} %w2_hbm.1, ...), custom_call_target="tpu_custom_call" | custom-call | tf_op jit(solution)/shard_map/pallas_call | solution.py:414
  53.3 1.7 %copy.9 = bf16[1,1,8,16,1024]{4,3,2,1,0:T(8,128)(2,1)} copy(bf16[1,1,8,16,1024]{4,3,2,1,0:T(8,128)(2,1)} %shard_map.73) | data formatting | bytes 524288
